TPU v7x, 32 devices: a whole 2x2x4 slice. The times are simulated.
32 devices in a mesh: seq: 16 (over z, x, core), head: 2 (over y).
Axes of the slice: x: 2, y: 2, z: 4, core: 2. Of those that a mesh axis runs over, the one named last changes fastest.
Arguments:
- queries: bfloat16 [4096, 4096], P('seq', 'head'), may hold values from -8 to 8
- keys: bfloat16 [4096, 4096], P('seq', 'head'), may hold values from -8 to 8
- values: bfloat16 [4096, 4096], P('seq', 'head'), may hold values from -6 to 6
- features: float32 [32, 128, 256], P('head'), may hold values from -6 to 6
- output_proj_weight: bfloat16 [4096, 4096], P('head', 'seq'), may hold values from -0.125 to 0.125
Outputs:
- mixed: bfloat16 [4096, 4096], P('seq', 'head')
All inputs are finite; a program needn't handle non-finite values.
Results may differ from a plain program's by a relative error of at most 0.005.
Values may be sent and summed in bfloat16 or wider, within the bound.
A program may use at most 192 MiB of HBM per device.

v0:
```python
import math
import jax
import jax.numpy as jnp
from jax import lax
from jax.sharding import PartitionSpec as P

DH = 128
M = 256
HIGH = lax.Precision.HIGHEST


def feature_map(x, direction):
    x = x * DH ** (-0.25)
    proj = jnp.einsum("htd,hdm->htm", x, direction, precision=HIGH)
    return jnp.exp(proj - 0.5 * jnp.sum(x * x, axis=-1, keepdims=True)) / math.sqrt(M)


def shards(queries, keys, values, features, output_proj_weight):
    tok_rows = queries.shape[0]
    local_heads = features.shape[0]
    devices, here = (lax.axis_size("seq"), lax.axis_index("seq"))
    halves, half = (lax.axis_size("head"), lax.axis_index("head"))

    def split_heads(arr):
        return arr.astype(jnp.float32).reshape(tok_rows, local_heads, DH).transpose(1, 0, 2)

    kf = feature_map(split_heads(keys), features)
    v = split_heads(values)
    v = jnp.concatenate([v, jnp.ones((local_heads, tok_rows, 8), jnp.float32)], axis=2)
    state = jnp.einsum("htp,htk->hpk", v, kf, precision=HIGH)
    states = lax.all_gather(state.astype(jnp.bfloat16), "seq")
    state, weight = lax.optimization_barrier((state, output_proj_weight))
    whole = lax.all_gather(weight, "seq", axis=1, tiled=True)
    qf = feature_map(split_heads(queries), features)
    lower = jnp.tril(jnp.ones((tok_rows, tok_rows), jnp.float32))
    scores = jnp.einsum("htm,hsm->hts", qf, kf, precision=HIGH) * lower
    both = jnp.einsum("hts,hsd->htd", scores, v, precision=HIGH)
    earlier = (jnp.arange(devices) < here)[:, None, None, None]
    prior = jnp.sum(jnp.where(earlier, states.astype(jnp.float32), 0.0), axis=0)
    both = both + jnp.einsum("htk,hpk->htp", qf, prior, precision=HIGH)
    attended = both[:, :, :DH] / both[:, :, DH : DH + 1]
    attended = attended.transpose(1, 0, 2).reshape(tok_rows, local_heads * DH).astype(jnp.bfloat16)
    partial = jnp.dot(attended, whole, preferred_element_type=jnp.float32)
    width = partial.shape[1] // halves
    total = lax.dynamic_slice_in_dim(partial, half * width, width, 1)
    for shift in range(1, halves):
        theirs = lax.rem(half + shift, halves)
        piece = lax.dynamic_slice_in_dim(partial, theirs * width, width, 1).astype(jnp.bfloat16)
        got = lax.ppermute(piece, "head", [(i, (i + shift) % halves) for i in range(halves)])
        total = total + got.astype(jnp.float32)
    return total.astype(jnp.bfloat16)


def solution(mesh):
    in_specs = (
        P("seq", "head"),
        P("seq", "head"),
        P("seq", "head"),
        P("head", None, None),
        P("head", "seq"),
    )
    return jax.shard_map(
        shards, mesh=mesh, in_specs=in_specs, out_specs=P("seq", "head"), check_vma=False
    )
```

profile of v0, /device:TPU:0, one launch (start us, length us, event | category | flops | bytes accessed | tf_op | source)
XLA Modules:
  0.0 298.5 jit_solution(12855215793351295603)
XLA Ops:
  6.5 0.0 all-gather.6.cloned.1.call-start
  6.5 2.0 fusion.8
  8.5 7.0 %fusion.7 = f32[16,256,256]{2,1,0:T(8,128)} fusion(f32[16,128,256]{2,1,0:T(8,128)S(1)} %copy-done, bf16[256,2048]{1,0:T(8,128)(2,1)} %param.6), kind=kOutput, calls=%fused_computation.11 | convolution fusion | flops 1611661312 | bytes 7340032 | tf_op jit(solution)/shard_map/htd,hdm->htm/dot_general | solution.py:14
  15.5 1.5 copy.11
  17.0 5.6 %fusion.5 = bf16[16,136,256]{2,1,0:T(8,128)(2,1)} fusion(f32[16,256,256]{2,1,0:T(8,128)} %fusion.7, f32[16,256]{1,0:T(8,128)S(1)} %broadcast_multiply_fusion, bf16[16,256,128]{1,2,0:T(8,128)(2,1)S(1)} %bitcast.55), kind=kOutput, calls=%fused_computation.8 | convolution fusion | flops 1713373184 | bytes 6373376 | tf_op jit(solution)/shard_map/htp,htk->hpk/dot_general | solution.py:30
  22.6 0.0 all-gather.6.cloned.1.call-update
  22.6 0.0 all-gather.4.cloned.1.call-start
  22.6 0.7 all-gather.4.cloned.1.call-update
  23.4 2.0 fusion.11
  25.4 4.9 %fusion.10 = f32[16,256,256]{2,1,0:T(8,128)S(1)} fusion(f32[16,128,256]{2,1,0:T(8,128)S(1)} %copy-done, bf16[256,2048]{1,0:T(8,128)(2,1)} %param.5), kind=kOutput, calls=%fused_computation.15 | convolution fusion | flops 1611661312 | bytes 7340032 | tf_op jit(solution)/shard_map/htd,hdm->htm/dot_general | solution.py:14
  30.3 2.0 copy-done.3
  32.3 7.0 %fusion.4 = f32[16,256,256]{2,1,0:T(8,128)} fusion(f32[16,256,256]{2,1,0:T(8,128)S(1)} %fusion.10, f32[16,256,256]{2,1,0:T(8,128)S(1)} %copy-done.2, f32[16,256]{1,0:T(8,128)S(1)} %broadcast_multiply_fusion, f32[16,256]{1,0:T(8,128)S(1)} %broadcast_multiply_fusion.1), kind=kOutput, calls=%fused_computation.7 | convolution fusion | flops 3225419776 | bytes 12615680 | tf_op jit(solution)/shard_map/htm,hsm->hts/dot_general | solution.py:36
  39.3 80.2 %all-gather.6.cloned.1.call-done = bf16[256,136,256]{2,1,0:T(8,128)(2,1)} async-done(((bf16[16,136,256]{2,1,0:T(8,128)(2,1)}), bf16[256,136,256]{2,1,0:T(8,128)(2,1)}) %all-gather.6.cloned.1.call-update) | async-done | bytes 17825808 | tf_op jit(solution)/shard_map/all_gather | solution.py:31
  119.5 11.7 %fusion = f32[16,136,256]{2,1,0:T(8,128)S(1)} fusion(bf16[16,16,136,256]{3,2,1,0:T(8,128)(2,1)} %bitcast.54, pred[16]{0:T(512)(128)(4,1)S(1)} %iota_compare_fusion.1), kind=kLoop, calls=%fused_computation.1 | loop fusion | flops 26181632 | bytes 20054032 | tf_op jit(solution)/shard_map/reduce_sum | solution.py:39
  131.2 5.5 %fusion.3 = f32[16,256,136]{1,2,0:T(8,128)S(1)} fusion(f32[16,136,256]{2,1,0:T(8,128)S(1)} %fusion, f32[16,256,256]{2,1,0:T(8,128)S(1)} %copy-done.4, f32[16,256]{1,0:T(8,128)S(1)} %broadcast_multiply_fusion.1), kind=kOutput, calls=%fused_computation.6 | convolution fusion | flops 1713373184 | bytes 8667136 | tf_op jit(solution)/shard_map/htk,hpk->htp/dot_general | solution.py:40
  136.6 2.7 fusion.23
  139.4 0.2 fusion.12
  139.7 112.3 %all-gather.4.cloned.1.call-done = bf16[2048,4096]{1,0:T(8,128)(2,1)} async-done(((bf16[2048,256]{1,0:T(8,128)(2,1)}), bf16[2048,4096]{1,0:T(8,128)(2,1)}) %all-gather.4.cloned.1.call-update) | async-done | bytes 16777232 | tf_op jit(solution)/shard_map/all_gather | solution.py:33
  252.0 8.3 %fusion.34 = f32[256,4096]{1,0:T(8,128)S(1)} fusion(bf16[256,2048]{0,1:T(8,128)(2,1)S(1)} %bitcast.57, bf16[2048,4096]{1,0:T(8,128)(2,1)} %all-gather.4.cloned.1.call-done), kind=kOutput, calls=%fused_computation.47 | convolution fusion | flops 4294967296 | bytes 22020096 | tf_op jit(solution)/shard_map/dot_general | solution.py:43
  260.3 1.9 copy-done.6
  262.2 1.1 dynamic-slice_convert_fusion
  263.3 1.5 collective-permute-start
  264.8 24.1 %collective-permute-done = bf16[256,2048]{1,0:T(8,128)(2,1)S(1)} collective-permute-done((bf16[256,2048]{1,0:T(8,128)(2,1)}, bf16[256,2048]{1,0:T(8,128)(2,1)S(1)}, u32[]{:S(2)}, u32[]{:S(2)}) %collective-permute-start) | collective-permute-done | bytes 1048608 | tf_op jit(solution)/shard_map/ppermute | solution.py:49
  288.9 2.9 add_convert_fusion
  (18 shorter events, 0.1 us)
Async XLA Ops:
  6.5 2.0 copy-start
  6.5 112.9 %all-gather.6.cloned.1.call-start = ((), (), s32[]{:S(2)}) async-start(), calls=%async_computation.1 | async-start | bytes 18939904 | tf_op jit(solution)/shard_map/all_gather | solution.py:31
  22.6 229.4 %all-gather.4.cloned.1.call-start = ((), (), s32[]{:S(2)}) async-start(), calls=%async_computation | async-start | bytes 17825792 | tf_op jit(solution)/shard_map/all_gather | solution.py:33
  23.4 9.0 %copy-start.2 = (f32[16,256,256]{2,1,0:T(8,128)S(1)}, f32[16,256,256]{2,1,0:T(8,128)}, u32[]{:S(2)}) copy-start(f32[16,256,256]{2,1,0:T(8,128)} %fusion.7) | copy-start | bytes 12582916
  30.3 2.0 copy-start.3
  119.5 11.7 %copy-start.4 = (f32[16,256,256]{2,1,0:T(8,128)S(1)}, f32[16,256,256]{2,1,0:T(8,128)}, u32[]{:S(2)}) copy-start(f32[16,256,256]{2,1,0:T(8,128)} %copy-done.3) | copy-start | bytes 12582916
  131.2 5.5 %copy-start.5 = (f32[16,256,256]{2,1,0:T(8,128)S(1)}, f32[16,256,256]{2,1,0:T(8,128)}, u32[]{:S(2)}) copy-start(f32[16,256,256]{2,1,0:T(8,128)} %fusion.4) | copy-start | bytes 12582916
  252.0 39.7 %copy-start.1 = (f32[16,128,256]{2,1,0:T(8,128)S(1)}, f32[16,128,256]{2,1,0:T(8,128)}, u32[]{:S(2)}) copy-start(f32[16,128,256]{2,1,0:T(8,128)} %param.8) | copy-start | bytes 6291460
  260.3 1.9 copy-start.6
  263.3 25.5 %collective-permute-start = (bf16[256,2048]{1,0:T(8,128)(2,1)}, bf16[256,2048]{1,0:T(8,128)(2,1)S(1)}, u32[]{:S(2)}, u32[]{:S(2)}) collective-permute-start(bf16[256,2048]{1,0:T(8,128)(2,1)} %dynamic-slice_convert_fusion), channel_id=1, source_target_pairs={{0,1},{1,0},{2,3},{3,2},{4,5},{5,4},{6,7},{7,6},{8,9},{9,8},{10,11... | collective-permute-start | bytes 3145736 | tf_op jit(solution)/shard_map/ppermute | solution.py:49
Sparse Core Ops, SparseCore 0:
  22.7 96.7 all-gather.5
  121.6 130.3 all-gather.3
where the time goes:
time: 299 us
  waiting for transfers between devices  217 us (73%)
  matrix products  40.9 us (14%)
  other arithmetic  18.8 us (6%)
  between operations  13.6 us (5%)
  local copies, waits for them, and re-layouts  6.56 us (2%)
    all_gather x1, waiting for transfers between devices, shards(): whole = lax.all_gather(weight, 'seq', axis=1, tiled=True)  112 us
    all_gather x1, waiting for transfers between devices, shards(): states = lax.all_gather(state.astype(jnp.bfloat16), 'seq')  80.2 us
    ppermute x1, waiting for transfers between devices, shards(): lax.ppermute(piece, 'head', [(i, (i + shift) % halves) for i in range(hal...  24.1 us
    dot_general x2, matrix products, feature_map(): proj = jnp.einsum('htd,hdm->htm', x, direction, precision=HIGH)  11.9 us
    reduce_sum x1, other arithmetic, shards(): prior = jnp.sum(jnp.where(earlier, states.astype(jnp.float32), 0.0), axis=0)  11.7 us
    dot_general x1, matrix products, shards(): partial = jnp.dot(attended, whole, preferred_element_type=jnp.float32)  8.28 us
    dot_general x1, matrix products, shards(): scores = jnp.einsum('htm,hsm->hts', qf, kf, precision=HIGH) * lower  6.97 us
  transfers between devices with their start and end apart: 3, of which 3 were waited for; matrix products, arithmetic and copies ran while one was open for 11% of the time, Pallas kernels for 0%

commit v1 on v0

--- a/solution.py
+++ b/solution.py
@@ -7,6 +7,18 @@
 DH = 128
 M = 256
 HIGH = lax.Precision.HIGHEST
+
+
+def gather_by_bits(array, axis, dim):
+    ways, here = (lax.axis_size(axis), lax.axis_index(axis))
+    grown, reach = (array, 1)
+    while reach < ways:
+        theirs = lax.ppermute(grown, axis, [(d, d ^ reach) for d in range(ways)])
+        mine_first = jnp.concatenate([grown, theirs], axis=dim)
+        theirs_first = jnp.concatenate([theirs, grown], axis=dim)
+        grown = jnp.where(here & reach == 0, mine_first, theirs_first)
+        reach = 2 * reach
+    return grown
 
 
 def feature_map(x, direction):
@@ -30,7 +42,7 @@
     state = jnp.einsum("htp,htk->hpk", v, kf, precision=HIGH)
     states = lax.all_gather(state.astype(jnp.bfloat16), "seq")
     state, weight = lax.optimization_barrier((state, output_proj_weight))
-    whole = lax.all_gather(weight, "seq", axis=1, tiled=True)
+    whole = gather_by_bits(weight, "seq", 1)
     qf = feature_map(split_heads(queries), features)
     lower = jnp.tril(jnp.ones((tok_rows, tok_rows), jnp.float32))
     scores = jnp.einsum("htm,hsm->hts", qf, kf, precision=HIGH) * lower

time: 299 us -> 674 us (2.25)
  waiting for transfers between devices: 217 us -> 555 us
  other arithmetic: 18.8 us -> 40.8 us
  matrix products: 40.9 us -> 48.4 us
  starting transfers between devices: 1.52 us -> 9.02 us
    ppermute x0 -> x4, waiting for transfers between devices: none -> 532 us  [gather_by_bits(): theirs = lax.ppermute(grown, axis, [(d, d ^ reach) for d in range(ways)])]
    all_gather x1 -> x0, waiting for transfers between devices: 112 us -> none  [shards(): whole = lax.all_gather(weight, 'seq', axis=1, tiled=True)]
    all_gather x1, waiting for transfers between devices: 80.2 us -> 0.01 us  [shards(): states = lax.all_gather(state.astype(jnp.bfloat16), 'seq')]
    select_n x0 -> x3, other arithmetic: none -> 22 us  [gather_by_bits(): grown = jnp.where(here & reach == 0, mine_first, theirs_first)]
    ppermute x0 -> x4, starting transfers between devices: none -> 7.57 us  [gather_by_bits(): theirs = lax.ppermute(grown, axis, [(d, d ^ reach) for d in range(ways)])]
    dot_general x1, matrix products: 8.28 us -> 15.8 us  [shards(): partial = jnp.dot(attended, whole, preferred_element_type=jnp.float32)]
  transfers between devices with their start and end apart: 3 -> 6, of which waited for: 3 -> 5; matrix products, arithmetic and copies ran while one was open for 11% -> 8% of each run, Pallas kernels for 0% -> 0%
where the time goes in v1:
time: 674 us; the launch traced here: 673 us
  waiting for transfers between devices  555 us (82%)
  matrix products  48.4 us (7%)
  other arithmetic  40.8 us (6%)
  between operations  13.6 us (2%)
  starting transfers between devices  9.02 us (1%)
    ppermute x4, waiting for transfers between devices, gather_by_bits(): theirs = lax.ppermute(grown, axis, [(d, d ^ reach) for d in range(ways)])  532 us
    ppermute x1, waiting for transfers between devices, shards(): lax.ppermute(piece, 'head', [(i, (i + shift) % halves) for i in range(hal...  23.2 us
    select_n x3, other arithmetic, gather_by_bits(): grown = jnp.where(here & reach == 0, mine_first, theirs_first)  22 us
    dot_general x1, matrix products, shards(): partial = jnp.dot(attended, whole, preferred_element_type=jnp.float32)  15.8 us
  transfers between devices with their start and end apart: 6, of which 5 were waited for; matrix products, arithmetic and copies ran while one was open for 8% of the time, Pallas kernels for 0%

profile of v1, /device:TPU:0, one launch (start us, length us, event | category | flops | bytes accessed | tf_op | source)
XLA Modules:
  0.0 673.5 jit_solution(7712596965594915769)
XLA Ops:
  6.5 2.0 fusion.15
  8.5 6.9 %fusion.14 = f32[16,256,256]{2,1,0:T(8,128)} fusion(f32[16,128,256]{2,1,0:T(8,128)S(1)} %copy-done, bf16[256,2048]{1,0:T(8,128)(2,1)} %param.6), kind=kOutput, calls=%fused_computation.21 | convolution fusion | flops 1611661312 | bytes 7340032 | tf_op jit(solution)/shard_map/htd,hdm->htm/dot_general | solution.py:26
  15.5 1.5 copy.11
  17.0 5.6 fusion.12
  23.1 2.6 collective-permute-done
  25.7 4.1 maximum_select_fusion.4
  29.9 2.9 collective-permute-start.1
  32.7 91.2 %collective-permute-done.1 = bf16[2048,512]{1,0:T(8,128)(2,1)} collective-permute-done((bf16[2048,512]{1,0:T(8,128)(2,1)}, bf16[2048,512]{1,0:T(8,128)(2,1)}, u32[]{:S(2)}, u32[]{:S(2)}) %collective-permute-start.1) | collective-permute-done | bytes 2097184 | tf_op jit(solution)/shard_map/ppermute | solution.py:16
  123.9 6.6 maximum_select_fusion.3
  130.5 113.8 %collective-permute-done.2 = bf16[2048,1024]{1,0:T(8,128)(2,1)} collective-permute-done((bf16[2048,1024]{1,0:T(8,128)(2,1)}, bf16[2048,1024]{1,0:T(8,128)(2,1)}, u32[]{:S(2)}, u32[]{:S(2)}) %collective-permute-start.2) | collective-permute-done | bytes 4194336 | tf_op jit(solution)/shard_map/ppermute | solution.py:16
  244.3 11.3 %maximum_select_fusion.2 = bf16[2048,2048]{1,0:T(8,128)(2,1)} fusion(bf16[2048,1024]{1,0:T(8,128)(2,1)} %collective-permute-done.2, bf16[2048,1024]{1,0:T(8,128)(2,1)} %maximum_select_fusion.3, pred[]{:T(512)S(6)} %eq.13), kind=kLoop, calls=%fused_computation.10 | loop fusion | flops 37748736 | bytes 16777216 | tf_op jit(solution)/shard_map/jit(_where)/select_n | solution.py:19
  255.7 4.2 collective-permute-start.3
  259.9 2.0 fusion.18
  261.9 4.9 fusion.17
  266.8 2.0 copy-done.3
  268.8 7.0 %fusion.11 = f32[16,256,256]{2,1,0:T(8,128)} fusion(f32[16,256,256]{2,1,0:T(8,128)S(1)} %fusion.17, f32[16,256,256]{2,1,0:T(8,128)S(1)} %copy-done.2, f32[16,256]{1,0:T(8,128)S(1)} %broadcast_multiply_fusion, f32[16,256]{1,0:T(8,128)S(1)} %broadcast_multiply_fusion.1), kind=kOutput, calls=%fused_computation.17 | convolution fusion | flops 3225419776 | bytes 12615680 | tf_op jit(solution)/shard_map/htm,hsm->hts/dot_general | solution.py:48
  275.8 11.6 %fusion = f32[16,136,256]{2,1,0:T(8,128)S(1)} fusion(bf16[16,16,136,256]{3,2,1,0:T(8,128)(2,1)} %bitcast.53, pred[16]{0:T(512)(128)(4,1)S(1)} %iota_compare_fusion.1), kind=kLoop, calls=%fused_computation.1 | loop fusion | flops 26181632 | bytes 20054032 | tf_op jit(solution)/shard_map/reduce_sum | solution.py:51
  287.4 5.5 fusion.10
  292.9 2.7 fusion.30
  295.9 324.3 %collective-permute-done.3 = bf16[2048,2048]{1,0:T(8,128)(2,1)} collective-permute-done((bf16[2048,2048]{1,0:T(8,128)(2,1)}, bf16[2048,2048]{1,0:T(8,128)(2,1)}, u32[]{:S(2)}, u32[]{:S(2)}) %collective-permute-start.3) | collective-permute-done | bytes 8388640 | tf_op jit(solution)/shard_map/ppermute | solution.py:16
  620.2 15.8 %fusion.1 = f32[256,4096]{1,0:T(8,128)S(1)} fusion(bf16[256,2048]{0,1:T(8,128)(2,1)S(1)} %bitcast.56, bf16[2048,2048]{1,0:T(8,128)(2,1)} %collective-permute-done.3, bf16[2048,2048]{1,0:T(8,128)(2,1)} %maximum_select_fusion.2, pred[]{:T(512)S(6)} %eq.12), kind=kOutput, calls=%fused_computation.3 | convolution fusion | flops 4370464768 | bytes 22020096 | tf_op jit(solution)/shard_map/dot_general | solution.py:55
  636.0 1.9 copy-done.6
  640.5 23.2 %collective-permute-done.4 = bf16[256,2048]{1,0:T(8,128)(2,1)S(1)} collective-permute-done((bf16[256,2048]{1,0:T(8,128)(2,1)}, bf16[256,2048]{1,0:T(8,128)(2,1)S(1)}, u32[]{:S(2)}, u32[]{:S(2)}) %collective-permute-start.4) | collective-permute-done | bytes 1048608 | tf_op jit(solution)/shard_map/ppermute | solution.py:61
  663.8 2.9 add_convert_fusion
  (26 shorter events, 3.4 us)
Async XLA Ops:
  6.5 2.0 copy-start
  6.5 269.2 %all-gather.3.cloned.1.call-start = ((), (), s32[]{:S(2)}) async-start(), calls=%async_computation | async-start | bytes 18939904 | tf_op jit(solution)/shard_map/all_gather | solution.py:43
  22.6 3.1 collective-permute-start
  29.9 94.1 %collective-permute-start.1 = (bf16[2048,512]{1,0:T(8,128)(2,1)}, bf16[2048,512]{1,0:T(8,128)(2,1)}, u32[]{:S(2)}, u32[]{:S(2)}) collective-permute-start(bf16[2048,512]{1,0:T(8,128)(2,1)} %maximum_select_fusion.4), channel_id=1, source_target_pairs={{0,4},{2,6},{4,0},{6,2},{8,12},{10,14},{12,8},{14,10},{16,20},{18,... | collective-permute-start | bytes 6291464 | tf_op jit(solution)/shard_map/ppermute | solution.py:16
  130.5 113.8 %collective-permute-start.2 = (bf16[2048,1024]{1,0:T(8,128)(2,1)}, bf16[2048,1024]{1,0:T(8,128)(2,1)}, u32[]{:S(2)}, u32[]{:S(2)}) collective-permute-start(bf16[2048,1024]{1,0:T(8,128)(2,1)} %maximum_select_fusion.3), channel_id=1, source_target_pairs={{0,8},{2,10},{4,12},{6,14},{8,0},{10,2},{12,4},{14,6},{16,24},{18,... | collective-permute-start | bytes 12582920 | tf_op jit(solution)/shard_map/ppermute | solution.py:16
  255.7 364.6 %collective-permute-start.3 = (bf16[2048,2048]{1,0:T(8,128)(2,1)}, bf16[2048,2048]{1,0:T(8,128)(2,1)}, u32[]{:S(2)}, u32[]{:S(2)}) collective-permute-start(bf16[2048,2048]{1,0:T(8,128)(2,1)} %maximum_select_fusion.2), channel_id=1, source_target_pairs={{0,16},{2,18},{4,20},{6,22},{8,24},{10,26},{12,28},{14,30},{16,0},... | collective-permute-start | bytes 25165832 | tf_op jit(solution)/shard_map/ppermute | solution.py:16
  259.9 8.9 %copy-start.2 = (f32[16,256,256]{2,1,0:T(8,128)S(1)}, f32[16,256,256]{2,1,0:T(8,128)}, u32[]{:S(2)}) copy-start(f32[16,256,256]{2,1,0:T(8,128)} %fusion.14) | copy-start | bytes 12582916
  266.8 2.0 copy-start.3
  275.8 11.7 %copy-start.4 = (f32[16,256,256]{2,1,0:T(8,128)S(1)}, f32[16,256,256]{2,1,0:T(8,128)}, u32[]{:S(2)}) copy-start(f32[16,256,256]{2,1,0:T(8,128)} %copy-done.3) | copy-start | bytes 12582916
  287.4 5.5 copy-start.5
  620.2 46.4 %copy-start.1 = (f32[16,128,256]{2,1,0:T(8,128)S(1)}, f32[16,128,256]{2,1,0:T(8,128)}, u32[]{:S(2)}) copy-start(f32[16,128,256]{2,1,0:T(8,128)} %param.8) | copy-start | bytes 6291460
  636.0 1.9 copy-start.6
  639.1 24.7 %collective-permute-start.4 = (bf16[256,2048]{1,0:T(8,128)(2,1)}, bf16[256,2048]{1,0:T(8,128)(2,1)S(1)}, u32[]{:S(2)}, u32[]{:S(2)}) collective-permute-start(bf16[256,2048]{1,0:T(8,128)(2,1)} %dynamic-slice_convert_fusion), channel_id=1, source_target_pairs={{0,1},{1,0},{2,3},{3,2},{4,5},{5,4},{6,7},{7,6},{8,9},{9,8},{10,11... | collective-permute-start | bytes 3145736 | tf_op jit(solution)/shard_map/ppermute | solution.py:61
Sparse Core Ops, SparseCore 0:
  22.7 155.4 all-gather.2
